TPU v7x, 32 devices: a whole 2x2x4 slice. The times are simulated.
32 devices in a mesh: scen: 16 (over z, y, core), net: 2 (over x).
Axes of the slice: x: 2, y: 2, z: 4, core: 2. Of those that a mesh axis runs over, the one named last changes fastest.
Arguments:
- generation: float32 [16, 168, 4096], P('scen', None, 'net'), may hold values from 0 to 2
- charging: float32 [16, 168, 1024], P('scen', None, 'net'), may hold values from 0 to 0.5
- discharging: float32 [16, 168, 1024], P('scen', None, 'net'), may hold values from 0 to 0.5
- plant_capacity: float32 [4096], P('net'), may hold values from 1 to 3
- store_capacity: float32 [1024], P('net'), may hold values from 4 to 12
- dual_balance: float32 [16, 168], P('scen'), may hold values from -6 to 6
- dual_line: float32 [16, 168, 8192], P('scen', None, 'net'), may hold values from -6 to 6
- dual_headroom: float32 [16, 168, 4096], P('scen', None, 'net'), may hold values from 0 to 1
- dual_empty: float32 [16, 168, 1024], P('scen', None, 'net'), may hold values from -1 to 0
- dual_full: float32 [16, 168, 1024], P('scen', None, 'net'), may hold values from 0 to 1
- availability: float32 [16, 168, 4096], P('scen', None, 'net'), may hold values from 0.1 to 1
- demand: float32 [16, 168], P('scen'), may hold values from 0.5 to 1.5
- line_base: float32 [16, 168, 8192], P('scen', None, 'net'), may hold values from -6 to 6
- line_limit: float32 [8192], P('net'), may hold values from 0.5 to 2
- fuel_cost: float32 [4096], P('net'), may hold values from 0.1 to 2
- plant_cost: float32 [4096], P('net'), may hold values from 0.1 to 1
- store_cost: float32 [1024], P('net'), may hold values from 0.05 to 0.5
- self_loss: float32 [1024], P('net'), may hold values from 0.002 to 0.05
- power_limit: float32 [1024], P('net'), may hold values from 0.5 to 2
- store_node: int32 [1024], P('net'), may hold values from 0 to 4095, as said below
- line_factors: float32 [16, 512, 10, 256], P('net', 'scen'), may hold values from -0.125 to 0.125
- block_pattern: int32 [16, 10], P('net'), may hold values from 0 to 15, as said below
Outputs:
- next_generation: float32 [16, 168, 4096], P('scen', None, 'net')
- next_charging: float32 [16, 168, 1024], P('scen', None, 'net')
- next_discharging: float32 [16, 168, 1024], P('scen', None, 'net')
- next_plant: float32 [4096], P('net')
- next_store: float32 [1024], P('net')
- next_balance: float32 [16, 168], P('scen')
- next_line: float32 [16, 168, 8192], P('scen', None, 'net')
- next_headroom: float32 [16, 168, 4096], P('scen', None, 'net')
- next_empty: float32 [16, 168, 1024], P('scen', None, 'net')
- next_full: float32 [16, 168, 1024], P('scen', None, 'net')
Inputs may be any that keep to these rules, and one draw needn't show every extreme that they name: `store_node`: storage unit k sits at a node of block k // 64. `block_pattern`: row b lists 10 different node blocks, the first of them b itself.
All inputs are finite; a program needn't handle non-finite values.
Results may differ from a plain program's by a relative error of at most 0.00016.
Values sent between devices are 32-bit elements; how exact they have to be, the bound alone decides.
A program may use at most 128 MiB of HBM per device.

v0:
```python
import jax
import jax.numpy as jnp
from jax import lax
from jax.sharding import PartitionSpec as P

DAY = 24


highest = lax.Precision.HIGHEST
primal_step = 0.5
dual_step = 0.5
store_step = 0.05
level_step = 0.05
efficiency = 0.92


def day_tables(self_loss):
    log_keep = jnp.log1p(-self_loss)
    within_day = jnp.arange(DAY, dtype=jnp.float32)
    lagged = within_day[:, None] - within_day[None, :]
    powers = jnp.exp(jnp.maximum(lagged, 0.0)[:, :, None] * log_keep[None, None, :])
    triangle = jnp.where(lagged[:, :, None] >= 0.0, powers, 0.0)
    carried = jnp.exp((within_day[:, None] + 1.0) * log_keep[None, :])
    return (triangle, carried)


def charge_levels(charge_drive, triangle, carried):
    scen_rows, hour_count, stores = charge_drive.shape
    day_count = hour_count // DAY
    blocked = charge_drive.reshape(scen_rows, day_count, DAY, stores)
    within = jnp.einsum("sduk,tuk->sdtk", blocked, triangle, precision=highest)
    current = jnp.zeros((scen_rows, stores), jnp.float32)
    results = []
    for day_index in range(day_count):
        filled = within[:, day_index] + carried[None] * current[:, None, :]
        results.append(filled)
        current = filled[:, DAY - 1]
    return jnp.concatenate(results, axis=1)


def charge_adjoint(weights, triangle, carried):
    scen_rows, hour_count, stores = weights.shape
    day_count = hour_count // DAY
    blocked = weights.reshape(scen_rows, day_count, DAY, stores)
    within = jnp.einsum("sdtk,tuk->sduk", blocked, triangle, precision=highest)
    back_carry = carried[::-1]
    current = jnp.zeros((scen_rows, stores), jnp.float32)
    results = []
    for day_index in reversed(range(day_count)):
        filled = within[:, day_index] + back_carry[None] * current[:, None, :]
        results.append(filled)
        current = filled[:, 0]
    return jnp.concatenate(results[::-1], axis=1)


def body(
    generation,
    charging,
    discharging,
    plant_capacity,
    store_capacity,
    dual_balance,
    dual_line,
    dual_headroom,
    dual_empty,
    dual_full,
    availability,
    demand,
    line_base,
    line_limit,
    fuel_cost,
    plant_cost,
    store_cost,
    self_loss,
    power_limit,
    store_node,
    line_factors,
    block_pattern,
):
    scen_rows, hour_count, node_local = generation.shape
    groups, lines_local, slot_count, block_width = line_factors.shape
    block_count = groups * lax.axis_size("net")
    line_group = lines_local * lax.axis_size("scen")
    grouped_duals = dual_line.reshape(scen_rows, hour_count, groups, line_group)
    block_marks = (
        block_pattern[:, :, None] == jnp.arange(block_count, dtype=jnp.int32)[None, None, :]
    ).astype(jnp.float32)
    full_factors = lax.all_gather(line_factors, "scen", axis=1, tiled=True)
    spread = jnp.einsum("shgl,glpc->shgpc", grouped_duals, full_factors, precision=highest)
    partial_value = jnp.einsum("shgpc,gpb->shbc", spread, block_marks, precision=highest)
    net_index = lax.axis_index("net")
    summed = lax.psum(partial_value, "net")
    own_blocks = lax.dynamic_slice_in_dim(summed, net_index * groups, groups, 2)
    line_image = own_blocks.reshape(scen_rows, hour_count, node_local)
    nodal_price = dual_balance[:, :, None] + line_image
    local_node = store_node - net_index * node_local
    locate = (local_node[:, None] == jnp.arange(node_local, dtype=jnp.int32)[None, :]).astype(
        jnp.float32
    )
    store_price = jnp.einsum("shn,kn->shk", nodal_price, locate, precision=highest)
    triangle, carried = day_tables(self_loss)
    backward = charge_adjoint(dual_empty + dual_full, triangle, carried)
    next_generation = jnp.maximum(
        generation - primal_step * (fuel_cost + nodal_price + dual_headroom), 0.0
    )
    next_charging = jnp.clip(
        charging - store_step * (efficiency * backward - store_price), 0.0, power_limit
    )
    next_discharging = jnp.clip(
        discharging - store_step * (store_price - backward / efficiency), 0.0, power_limit
    )
    plant_part = jnp.sum(availability * dual_headroom, axis=(0, 1))
    store_part = jnp.sum(dual_full, axis=(0, 1))
    plant_total, store_total = lax.psum((plant_part, store_part), "scen")
    scen_hours = scen_rows * lax.axis_size("scen") * hour_count
    next_plant = jnp.maximum(
        plant_capacity - primal_step * (plant_cost - plant_total / scen_hours), 0.0
    )
    next_store = jnp.maximum(
        store_capacity - primal_step * (store_cost - store_total / scen_hours), 0.0
    )
    extra_generation = 2.0 * next_generation - generation
    extra_charging = 2.0 * next_charging - charging
    extra_discharging = 2.0 * next_discharging - discharging
    extra_plant = 2.0 * next_plant - plant_capacity
    extra_store = 2.0 * next_store - store_capacity
    injection = extra_generation + jnp.einsum(
        "shk,kn->shn", extra_discharging - extra_charging, locate, precision=highest
    )
    all_injection = lax.all_gather(injection, "net", axis=2, tiled=True)
    total_injection = lax.psum(jnp.sum(injection, axis=2), "net")
    next_balance = dual_balance + dual_step * (
        total_injection / (block_count * block_width) - demand
    )
    all_blocks = all_injection.reshape(scen_rows, hour_count, block_count, block_width)
    chosen = jnp.take(all_blocks, block_pattern, axis=2)
    line_flows = jnp.einsum("shgpc,glpc->shgl", chosen, full_factors, precision=highest)
    line_flows = line_flows.reshape(scen_rows, hour_count, groups * line_group)
    line_moved = dual_line + dual_step * line_flows
    next_line = line_moved - dual_step * jnp.clip(
        line_moved / dual_step, -line_limit - line_base, line_limit - line_base
    )
    next_headroom = jnp.maximum(
        dual_headroom + dual_step * (extra_generation - availability * extra_plant), 0.0
    )
    levels = charge_levels(
        efficiency * extra_charging - extra_discharging / efficiency, triangle, carried
    )
    next_empty = jnp.minimum(dual_empty + level_step * levels, 0.0)
    next_full = jnp.maximum(dual_full + level_step * (levels - extra_store), 0.0)
    return (
        next_generation,
        next_charging,
        next_discharging,
        next_plant,
        next_store,
        next_balance,
        next_line,
        next_headroom,
        next_empty,
        next_full,
    )


def solution(mesh):
    placed = (
        P("scen", None, "net"),
        P("scen", None, "net"),
        P("scen", None, "net"),
        P("net"),
        P("net"),
        P("scen", None),
        P("scen", None, "net"),
        P("scen", None, "net"),
        P("scen", None, "net"),
        P("scen", None, "net"),
        P("scen", None, "net"),
        P("scen", None),
        P("scen", None, "net"),
        P("net"),
        P("net"),
        P("net"),
        P("net"),
        P("net"),
        P("net"),
        P("net"),
        P("net", "scen", None, None),
        P("net", None),
    )
    return jax.shard_map(
        body,
        mesh=mesh,
        in_specs=placed,
        out_specs=(
            P("scen", None, "net"),
            P("scen", None, "net"),
            P("scen", None, "net"),
            P("net"),
            P("net"),
            P("scen", None),
            P("scen", None, "net"),
            P("scen", None, "net"),
            P("scen", None, "net"),
            P("scen", None, "net"),
        ),
        check_vma=False,
    )
```

profile of v0, /device:TPU:0, one launch (start us, length us, event | category | flops | bytes accessed | tf_op | source)
XLA Modules:
  0.0 475.1 jit_solution(17177092378376315044)
XLA Ops:
  8.0 4.1 copy.94
  12.1 2.0 copy.67
  14.1 2.0 copy.65
  16.1 2.0 copy.76
  18.0 1.0 copy.75
  19.1 1.9 fusion.65
  21.0 1.9 copy.57
  24.2 8.2 %fusion.30 = f32[1,7,24,512]{2,1,3,0:T(8,128)S(1)} fusion(f32[7,24,512]{1,0,2:T(8,128)} %copy.57, f32[512]{0:T(512)S(1)} %negate_log-plus-one_fusion, f32[24,24]{1,0:T(8,128)S(1)} %fusion.56, pred[24,24]{1,0:T(8,128)(4,1)S(1)} %fusion.57), kind=kOutput, calls=%fused_computation.33 | convolution fusion | flops 25362432 | bytes 693056 | tf_op jit(solution)/shard_map/sdtk,tuk->sduk/dot_general | solution.py:45
  32.5 2.2 fusion.64
  35.2 184.6 %all-gather.3.cloned.1.call-done = f32[8,512,10,256]{3,1,2,0:T(8,128)} async-done(((f32[8,32,10,256]{3,1,2,0:T(8,128)}), f32[8,512,10,256]{3,1,2,0:T(8,128)}) %all-gather.3.cloned.1.call-update) | async-done | bytes 41943056 | tf_op jit(solution)/shard_map/all_gather | solution.py:88
  219.8 38.5 %convolution_bitcast_fusion = f32[168,8,10,256]{3,0,2,1:T(8,128)S(1)} fusion(f32[8,512,10,256]{3,1,2,0:T(8,128)} %all-gather.3.cloned.1.call-done, f32[168,8,512,1]{2,1,0,3:T(8,128)S(1)} %bitcast.172), kind=kOutput, calls=%fused_computation.6 | convolution fusion | flops 21139292160 | bytes 58458112 | tf_op jit(solution)/shard_map/shgl,glpc->shgpc/dot_general | solution.py:89
  258.3 14.4 %fusion.25 = f32[1,168,16,256]{3,2,1,0:T(8,128)} fusion(f32[168,8,10,256]{3,0,2,1:T(8,128)S(1)} %convolution_bitcast_fusion, s32[8,10]{1,0:T(8,128)S(1)} %copy-done.21), kind=kOutput, calls=%fused_computation.32 | convolution fusion | flops 660604160 | bytes 16515392 | tf_op jit(solution)/shard_map/shgpc,gpb->shbc/dot_general | solution.py:90
  275.4 1.2 multiply_add_fusion.2
  277.5 1.2 multiply_add_fusion.1
  280.4 2.5 concatenate.38
  283.8 60.8 %all-reduce = (f32[2048]{0:T(1024)S(1)}, f32[512]{0:T(512)S(1)}) all-reduce(f32[2048]{0:T(1024)S(1)} %multiply_reduce_fusion, f32[512]{0:T(512)S(1)} %copy-done.27), channel_id=1, replica_groups=mesh['scen'=16,'net'=2] {'scen'}, use_global_device_ids=true, to_apply=%region_2.3 | all-reduce | flops 2560 | bytes 20480 | tf_op jit(solution)/shard_map/psum | solution.py:114
  345.3 4.8 %all-reduce.3.cloned.1.call-done = f32[1,168,16,256]{3,2,1,0:T(8,128)} async-done(((f32[1,168,16,256]{3,2,1,0:T(8,128)}), f32[1,168,16,256]{3,2,1,0:T(8,128)}) %all-reduce.3.cloned.1.call-update) | async-done | bytes 2752528 | tf_op jit(solution)/shard_map/psum | solution.py:92
  350.2 1.4 constant_dynamic-slice_fusion
  351.6 1.3 reshape.1850
  354.7 3.2 add_maximum_fusion
  357.9 2.5 multiply_subtract_fusion.2
  360.5 3.1 fusion.66
  364.4 0.9 copy.77
  367.2 11.0 %fusion.7 = f32[512,24,7]{1,2,0:T(8,128)S(1)} fusion(f32[7,24,512]{1,0,2:T(8,128)S(1)} %copy.73, f32[512]{0:T(512)S(1)} %copy-done.24, f32[24,24]{1,0:T(8,128)S(1)} %copy-done.26, pred[24,24]{1,0:T(8,128)(4,1)S(1)} %copy-done.35), kind=kOutput, calls=%fused_computation.10 | convolution fusion | flops 25362432 | bytes 693056 | tf_op jit(solution)/shard_map/sduk,tuk->sdtk/dot_general | solution.py:31
  384.2 5.1 %psum.31 = f32[1,168]{1,0:T(1,128)S(1)} all-reduce(f32[1,168]{1,0:T(1,128)S(1)} %bitcast.193), channel_id=1, replica_groups=mesh['scen'=16,'net'=2] {'net'}, use_global_device_ids=true, to_apply=%region_6.7 | all-reduce | flops 168 | bytes 1344 | tf_op jit(solution)/shard_map/psum | solution.py:131
  389.9 14.4 %all-gather.5.cloned.1.call-done = f32[1,168,4096]{2,1,0:T(8,128)} async-done(((f32[1,168,2048]{2,1,0:T(8,128)}), f32[1,168,4096]{2,1,0:T(8,128)}) %all-gather.5.cloned.1.call-update) | async-done | bytes 2752528 | tf_op jit(solution)/shard_map/all_gather | solution.py:130
  404.3 2.8 copy.96
  407.1 1.6 copy.70
  408.7 6.3 %gather_fusion = f32[80,168,256]{2,1,0:T(8,128)} fusion(f32[168,16,256]{2,0,1:T(8,128)S(1)} %copy.70, s32[1024]{0:T(1024)S(1)} %pad_clamp_fusion), kind=kCustom, calls=%fused_computation | custom fusion | bytes 27525440 | tf_op jit(solution)/shard_map/jit(_take)/gather | solution.py:136
  415.1 48.1 %fusion.19 = f32[1,8,21,8,512]{4,3,2,1,0:T(8,128)S(1)} fusion(f32[8,512,10,256]{3,1,2,0:T(8,128)} %all-gather.3.cloned.1.call-done, f32[8,10,168,256]{3,2,1,0:T(8,128)} %bitcast.168, pred[8,10]{1,0:T(8,128)(4,1)S(1)} %compare_and_fusion), kind=kOutput, calls=%fused_computation.24 | convolution fusion | flops 21143420928 | bytes 58458192 | tf_op jit(solution)/shard_map/shgpc,glpc->shgl/dot_general | solution.py:137
  463.5 1.5 copy-done
  465.8 2.4 multiply_subtract_fusion
  (135 shorter events, 21.3 us)
Async XLA Ops:
  7.2 212.7 %all-gather.3.cloned.1.call-start = ((), (), s32[]{:S(2)}) async-start(), calls=%async_computation | async-start | bytes 44564480 | tf_op jit(solution)/shard_map/all_gather | solution.py:88
  7.9 342.3 %all-reduce.3.cloned.1.call-start = ((), (), s32[]{:S(2)}) async-start(), calls=%async_computation.1 | async-start | bytes 5505024 | tf_op jit(solution)/shard_map/psum | solution.py:92
  8.0 10.1 %copy-start.15 = (f32[1,168,512]{2,1,0:T(8,128)S(1)}, f32[1,168,512]{2,1,0:T(8,128)}, u32[]{:S(2)}) copy-start(f32[1,168,512]{2,1,0:T(8,128)} %param.30) | copy-start | bytes 1032196
  16.1 6.9 %copy-start.38 = (f32[512]{0:T(512)S(1)}, f32[512]{0:T(512)}, u32[]{:S(2)}) copy-start(f32[512]{0:T(512)} %param.39) | copy-start | bytes 6148
  23.4 9.0 %copy-start.23 = (f32[512]{0:T(512)}, f32[512]{0:T(512)S(1)}, u32[]{:S(2)}) copy-start(f32[512]{0:T(512)S(1)} %negate_log-plus-one_fusion) | copy-start | bytes 6148
  24.2 8.3 %copy-start.34 = (pred[24,24]{1,0:T(8,128)(4,1)}, pred[24,24]{1,0:T(8,128)(4,1)S(1)}, u32[]{:S(2)}) copy-start(pred[24,24]{1,0:T(8,128)(4,1)S(1)} %fusion.57) | copy-start | bytes 1732
  24.2 8.3 %copy-start.25 = (f32[24,24]{1,0:T(8,128)}, f32[24,24]{1,0:T(8,128)S(1)}, u32[]{:S(2)}) copy-start(f32[24,24]{1,0:T(8,128)S(1)} %fusion.56) | copy-start | bytes 6916
  219.8 38.5 %copy-start.21 = (s32[8,10]{1,0:T(8,128)S(1)}, s32[8,10]{1,0:T(8,128)}, u32[]{:S(2)}) copy-start(s32[8,10]{1,0:T(8,128)} %param.43) | copy-start | bytes 964
  272.8 131.6 %all-gather.5.cloned.1.call-start = ((), (), s32[]{:S(2)}) async-start(), calls=%async_computation.2 | async-start | bytes 4128768 | tf_op jit(solution)/shard_map/all_gather | solution.py:130
  272.8 6.7 %copy-start.16 = (f32[1,1,24,512]{2,1,3,0:T(1,128)S(1)}, f32[1,1,24,512]{2,1,3,0:T(1,128)}, u32[]{:S(2)}) copy-start(f32[1,1,24,512]{2,1,3,0:T(1,128)} %get-tuple-element.46) | copy-start | bytes 147460
  275.2 8.4 %copy-start.20 = (f32[4096]{0:T(1024)S(1)}, f32[4096]{0:T(1024)}, u32[]{:S(2)}) copy-start(f32[4096]{0:T(1024)} %param.35) | copy-start | bytes 49156
  275.2 8.4 %copy-start.1 = (f32[1,168,2048]{2,1,0:T(8,128)S(1)}, f32[1,168,2048]{2,1,0:T(8,128)}, u32[]{:S(2)}) copy-start(f32[1,168,2048]{2,1,0:T(8,128)} %param.29) | copy-start | bytes 4128772
  275.3 8.4 %copy-start.2 = (f32[1,168,2048]{2,1,0:T(8,128)S(1)}, f32[1,168,2048]{2,1,0:T(8,128)}, u32[]{:S(2)}) copy-start(f32[1,168,2048]{2,1,0:T(8,128)} %param.32) | copy-start | bytes 4128772
  280.4 3.5 copy-start.27
  280.4 64.3 %copy-start.39 = (s32[512]{0:T(512)S(1)}, s32[512]{0:T(512)}, u32[]{:S(2)}) copy-start(s32[512]{0:T(512)} %param.41) | copy-start | bytes 6148
  280.4 64.3 %copy-start.22 = (s32[8,10]{1,0:T(8,128)S(1)}, s32[8,10]{1,0:T(8,128)}, u32[]{:S(2)}) copy-start(s32[8,10]{1,0:T(8,128)} %param.43) | copy-start | bytes 964
  280.4 64.3 %copy-start.28 = (f32[2048]{0:T(1024)S(1)}, f32[2048]{0:T(1024)}, u32[]{:S(2)}) copy-start(f32[2048]{0:T(1024)} %param.25) | copy-start | bytes 24580
  280.4 64.3 %copy-start.29 = (f32[2048]{0:T(1024)S(1)}, f32[2048]{0:T(1024)}, u32[]{:S(2)}) copy-start(f32[2048]{0:T(1024)} %param.37) | copy-start | bytes 24580
  351.6 1.8 copy-start.30
  354.7 3.3 copy-start.11
  354.7 3.3 copy-start.12
  354.7 3.3 copy-start.19
  354.7 3.3 copy-start.41
  357.9 2.6 copy-start.5
  360.5 3.2 copy-start.36
  360.5 3.2 copy-start.37
  360.5 3.8 copy-start.24
  360.5 3.8 copy-start.32
  363.6 3.5 copy-start.26
  363.6 3.5 copy-start.35
  382.2 7.1 %copy-start.40 = (f32[1,168]{1,0:T(1,128)S(1)}, f32[1,168]{1,0:T(1,128)}, u32[]{:S(2)}) copy-start(f32[1,168]{1,0:T(1,128)} %param.33) | copy-start | bytes 2020
  463.2 2.6 copy-start.6
  (13 other events, 15.0 us)
Sparse Core Ops, SparseCore 0:
  9.5 210.2 all-gather.2
  272.9 77.2 all-reduce.2
  363.8 40.5 all-gather.4
where the time goes:
time: 479 us; the launch traced here: 475 us
  waiting for transfers between devices  205 us (43%)
  matrix products  126 us (26%)
  blocking collectives  65.9 us (14%)
  local copies, waits for them, and re-layouts  46.8 us (10%)
  other arithmetic  17.1 us (4%)
  between operations  14.8 us (3%)
    all_gather x1, waiting for transfers between devices, body(): full_factors = lax.all_gather(line_factors, 'scen', axis=1, tiled=True)  185 us
    psum x1, blocking collectives, body(): plant_total, store_total = lax.psum((plant_part, store_part), 'scen')  60.8 us
    dot_general x1, matrix products, body(): jnp.einsum('shgpc,glpc->shgl', chosen, full_factors, precision=highest)  48.1 us
    dot_general x1, matrix products, body(): jnp.einsum('shgl,glpc->shgpc', grouped_duals, full_factors, precision=hig...  38.5 us
    unnamed x95, local copies, waits for them, and re-layouts  25.5 us
    all_gather x1, waiting for transfers between devices, body(): all_injection = lax.all_gather(injection, 'net', axis=2, tiled=True)  14.4 us
    dot_general x1, matrix products, body(): jnp.einsum('shgpc,gpb->shbc', spread, block_marks, precision=highest)  14.4 us
    dot_general x1, matrix products, charge_levels(): within = jnp.einsum('sduk,tuk->sdtk', blocked, triangle, precision=highest)  11 us
  transfers between devices with their start and end apart: 3, of which 3 were waited for; matrix products, arithmetic and copies ran while one was open for 12% of the time, Pallas kernels for 0%

commit v1 on v0

v1 whole, which is shorter than its diff:
```python
import functools

import jax
import jax.numpy as jnp
from jax import lax
from jax.experimental import pallas as pl
from jax.experimental.pallas import tpu as pltpu
from jax.sharding import PartitionSpec as P

LANES = 128
primal_step = 0.5
dual_step = 0.5
store_step = 0.05
level_step = 0.05
efficiency = 0.92
f32 = jnp.float32
bf16 = jnp.bfloat16
VMEM_BYTES = 56 * 1024 * 1024


def split(x):
    hi = x.astype(bf16)
    return hi, (x - hi.astype(f32)).astype(bf16)


def stacked(x):
    return jnp.concatenate([x, x - x.astype(bf16).astype(f32)], axis=0).astype(bf16)


def dot(a, b):
    return jnp.dot(a, b, preferred_element_type=f32)


def dot_t(a, b):
    return lax.dot_general(a, b, (((1,), (1,)), ((), ())), preferred_element_type=f32)


def slot_steps(slots):
    return [range(j, min(j + 2, slots)) for j in range(0, slots, 2)]


def image_kernel(slots, parts, pat, dual, fac, *refs):
    outs, acc = refs[-1 - parts : -1], refs[-1]
    g = pl.program_id(0)
    hours = dual.shape[0]
    lines = fac.shape[0] * fac.shape[2]

    @pl.when(g == 0)
    def _():
        acc[...] = jnp.zeros_like(acc)

    both = stacked(dual[...])
    hi = dual[...].astype(bf16)
    for js in slot_steps(slots):
        w = fac[:, 0, :, js[0] * LANES : (js[-1] + 1) * LANES].reshape(lines, len(js) * LANES)
        wh, wl = split(w)
        r = dot(both, wh)
        r = r[:hours] + r[hours:] + dot(hi, wl)
        for i, j in enumerate(js):
            b = pat[g, j]
            acc[b] = acc[b] + r[:, i * LANES : (i + 1) * LANES]

    @pl.when(g == pl.num_programs(0) - 1)
    def _():
        own = outs[0].shape[0]
        for s in range(parts):
            outs[s][...] = acc[s * own : (s + 1) * own]


def image_parts(pattern, dual, fac, parts, after):
    groups, slots = pattern.shape
    hours = dual.shape[0]
    scen, _, lines_local, width = fac.shape
    lines = scen * lines_local
    full = jax.ShapeDtypeStruct((groups, hours, LANES), f32)
    whole = pl.BlockSpec((groups, hours, LANES), lambda g, pat: (0, 0, 0))
    return pl.pallas_call(
        functools.partial(image_kernel, slots, parts),
        out_shape=[full] * parts,
        grid_spec=pltpu.PrefetchScalarGridSpec(
            num_scalar_prefetch=1,
            grid=(groups,),
            in_specs=[
                pl.BlockSpec((hours, lines), lambda g, pat: (0, g)),
                pl.BlockSpec((scen, 1, lines_local, width), lambda g, pat: (0, g, 0, 0)),
            ]
            + [pl.BlockSpec(memory_space=pl.ANY)] * len(after),
            out_specs=[whole] * parts,
            scratch_shapes=[pltpu.VMEM((groups * parts, hours, LANES), f32)],
        ),
        compiler_params=pltpu.CompilerParams(vmem_limit_bytes=VMEM_BYTES),
        cost_estimate=pl.CostEstimate(
            flops=6 * groups * hours * lines * width,
            bytes_accessed=4 * groups * lines * width,
            transcendentals=0,
        ),
        name="image",
    )(pattern, dual, fac, *after)


def flow_kernel(slots, parts, first, last, pat, fac, *refs):
    injs, refs = refs[:parts], refs[parts:]
    if not first:
        prev, refs = refs[0], refs[1:]
    if last:
        dual, base, limit = refs[:3]
        refs = refs[3:]
    out, total, held = refs
    g = pl.program_id(0)
    own, hours, _ = injs[0].shape
    lines = fac.shape[0] * fac.shape[2]

    @pl.when(g == 0)
    def _():
        rows = jnp.zeros((hours, LANES), f32)
        for s in range(parts):
            for b in range(own):
                x = injs[s][b]
                held[s * own + b] = stacked(x)
                rows = rows + x
        total[...] = rows

    flows = jnp.zeros((hours, lines), f32) if first else prev[...]
    for js in slot_steps(slots):
        w = fac[:, 0, :, js[0] * LANES : (js[-1] + 1) * LANES].reshape(lines, len(js) * LANES)
        wh, wl = split(w)
        both = jnp.concatenate([held[pat[g, j]] for j in js], axis=1)
        hi = jnp.concatenate([held[pat[g, j], :hours] for j in js], axis=1)
        r = dot_t(both, wh)
        flows = flows + (r[:hours] + r[hours:] + dot_t(hi, wl))
    if last:
        moved = dual[...] + dual_step * flows
        low = -limit[...] - base[...]
        high = limit[...] - base[...]
        out[...] = moved - dual_step * jnp.minimum(jnp.maximum(moved / dual_step, low), high)
    else:
        out[...] = flows


def flow_step(pattern, fac, injs, prev, tail):
    groups, slots = pattern.shape
    parts = len(injs)
    hours = injs[0].shape[1]
    scen, _, lines_local, width = fac.shape
    lines = scen * lines_local
    by_group = pl.BlockSpec((hours, lines), lambda g, pat: (0, g))
    whole = pl.BlockSpec((groups, hours, LANES), lambda g, pat: (0, 0, 0))
    operands = list(injs)
    specs = [whole] * parts
    if prev is not None:
        operands.append(prev)
        specs.append(by_group)
    if tail is not None:
        operands += list(tail)
        specs += [by_group, by_group, pl.BlockSpec((1, lines), lambda g, pat: (0, g))]
    return pl.pallas_call(
        functools.partial(flow_kernel, slots, parts, prev is None, tail is not None),
        out_shape=[
            jax.ShapeDtypeStruct((hours, groups * lines), f32),
            jax.ShapeDtypeStruct((hours, LANES), f32),
        ],
        grid_spec=pltpu.PrefetchScalarGridSpec(
            num_scalar_prefetch=1,
            grid=(groups,),
            in_specs=[
                pl.BlockSpec((scen, 1, lines_local, width), lambda g, pat: (0, g, 0, 0)),
            ]
            + specs,
            out_specs=[by_group, pl.BlockSpec((hours, LANES), lambda g, pat: (0, 0))],
            scratch_shapes=[pltpu.VMEM((groups * parts, 2 * hours, LANES), bf16)],
        ),
        compiler_params=pltpu.CompilerParams(vmem_limit_bytes=VMEM_BYTES),
        cost_estimate=pl.CostEstimate(
            flops=6 * groups * hours * lines * width,
            bytes_accessed=4 * groups * lines * width,
            transcendentals=0,
        ),
        name="flows",
    )(pattern, fac, *operands)


def decayed_sums(x, keep, reverse):
    hours = x.shape[0]
    hour = lax.broadcasted_iota(jnp.int32, x.shape, 0)
    power = keep
    lag = 1
    while lag < hours:
        if reverse:
            moved = jnp.where(hour < hours - lag, pltpu.roll(x, hours - lag, 0), 0.0)
        else:
            moved = jnp.where(hour >= lag, pltpu.roll(x, lag, 0), 0.0)
        x = x + power * moved
        power = power * power
        lag *= 2
    return x


def adjoint_kernel(empty, full, loss, out):
    out[...] = decayed_sums(empty[...] + full[...], 1.0 - loss[...], True)


def level_kernel(charging, discharging, next_c, next_d, empty, full, loss, extra, out_e, out_f):
    extra_c = 2.0 * next_c[...] - charging[...]
    extra_d = 2.0 * next_d[...] - discharging[...]
    drive = efficiency * extra_c - extra_d / efficiency
    levels = decayed_sums(drive, 1.0 - loss[...], False)
    out_e[...] = jnp.minimum(empty[...] + level_step * levels, 0.0)
    out_f[...] = jnp.maximum(full[...] + level_step * (levels - extra[...]), 0.0)


def simple_call(kernel, out_shape, name, *operands):
    moved = sum(4 * x.size for x in operands) + sum(
        4 * x.size for x in jax.tree.leaves(out_shape)
    )
    return pl.pallas_call(
        kernel,
        out_shape=out_shape,
        compiler_params=pltpu.CompilerParams(vmem_limit_bytes=VMEM_BYTES),
        cost_estimate=pl.CostEstimate(flops=8 * moved, bytes_accessed=moved, transcendentals=0),
        name=name,
    )(*operands)


def dispatch_kernel(chunk, width, parts, store_blk, *refs):
    images, refs = refs[:parts], refs[parts:]
    (balance, generation, headroom, fuel, charging, discharging, backward, power, rows,
     price_in, gen_in, gen_out, inj, price_out, out_c, out_d) = refs
    groups = images[0].shape[0]
    per = LANES // store_blk
    gen_out[...] = gen_in[...]
    for t in range(groups // per):
        prices, extras = [], []
        for b in range(t * per, (t + 1) * per):
            cols = slice(b * width + chunk * LANES, b * width + (chunk + 1) * LANES)
            image = images[0][b]
            for other in images[1:]:
                image = image + other[b]
            price = balance[...] + image
            gen = generation[:, cols]
            moved = jnp.maximum(gen - primal_step * (fuel[:, cols] + price + headroom[:, cols]), 0.0)
            gen_out[:, cols] = moved
            prices.append(price)
            extras.append(2.0 * moved - gen)
        units = slice(t * LANES, (t + 1) * LANES)
        place = lax.broadcasted_iota(jnp.int32, (per * LANES, LANES), 0)
        marks = jnp.where(place == rows[:, units], 1.0, 0.0).astype(bf16)
        hi, lo = split(jnp.concatenate(prices, axis=1))
        price = price_in[:, units] + (dot(hi, marks) + dot(lo, marks))
        price_out[:, units] = price
        back = backward[:, units]
        cap = power[:, units]
        c, d = charging[:, units], discharging[:, units]
        next_c = jnp.minimum(jnp.maximum(c - store_step * (efficiency * back - price), 0.0), cap)
        next_d = jnp.minimum(jnp.maximum(d - store_step * (price - back / efficiency), 0.0), cap)
        out_c[:, units] = next_c
        out_d[:, units] = next_d
        hi, lo = split((2.0 * next_d - d) - (2.0 * next_c - c))
        spread = dot_t(hi, marks) + dot_t(lo, marks)
        for i in range(per):
            inj[t * per + i] = extras[i] + spread[:, i * LANES : (i + 1) * LANES]


def body(
    generation, charging, discharging, plant_capacity, store_capacity, dual_balance, dual_line,
    dual_headroom, dual_empty, dual_full, availability, demand, line_base, line_limit, fuel_cost,
    plant_cost, store_cost, self_loss, power_limit, store_node, line_factors, block_pattern,
):
    scen_rows, hours, node_local = generation.shape
    groups, lines_local, slots, width = line_factors.shape
    parts = lax.axis_size("net")
    scen_size = lax.axis_size("scen")
    block_count = groups * parts
    stores = store_node.shape[0]
    store_blk = stores // groups
    chunks = width // LANES
    me = lax.axis_index("net")

    gen, chg, dis = generation[0], charging[0], discharging[0]
    line, head = dual_line[0], dual_headroom[0]
    empty, full, avail = dual_empty[0], dual_full[0], availability[0]
    loss = self_loss[None, :]

    pattern = (block_pattern - me * groups + block_count) % block_count
    node = store_node - me * node_local
    unit = jnp.arange(stores, dtype=jnp.int32)
    per = LANES // store_blk
    pair_row = (node // width - (unit // LANES) * per) * LANES + node % LANES
    gathered = []
    for q in range(chunks):
        piece = line_factors[:, :, :, q * LANES : (q + 1) * LANES]
        piece = piece.reshape(groups, lines_local, slots * LANES)
        gathered.append(lax.all_gather(piece, "scen", axis=0))

    backward = simple_call(
        adjoint_kernel, jax.ShapeDtypeStruct((hours, stores), f32), "adjoint", empty, full, loss
    )
    plant_part = jnp.sum(avail * head, axis=0)
    store_part = jnp.sum(full, axis=0)
    totals = lax.psum(jnp.concatenate([plant_part, store_part]), "scen")
    plant_total, store_total = totals[:node_local], totals[node_local:]
    scen_hours = scen_rows * scen_size * hours
    next_plant = jnp.maximum(
        plant_capacity - primal_step * (plant_cost - plant_total / scen_hours), 0.0
    )
    next_store = jnp.maximum(
        store_capacity - primal_step * (store_cost - store_total / scen_hours), 0.0
    )
    extra_plant = 2.0 * next_plant - plant_capacity
    extra_store = 2.0 * next_store - store_capacity

    price = jnp.zeros((hours, stores), f32)
    next_gen = gen
    flows = None
    totals_by_lane = jnp.zeros((hours, LANES), f32)
    by_store = jax.ShapeDtypeStruct((hours, stores), f32)
    by_node = jax.ShapeDtypeStruct((hours, node_local), f32)
    for q in range(chunks):
        after = [totals, backward] if q == 0 else [flows]
        partial_images = image_parts(pattern, line, gathered[q], parts, after)
        images = [partial_images[0]]
        for s in range(1, parts):
            images.append(
                lax.ppermute(partial_images[s], "net", [(i, (i + s) % parts) for i in range(parts)])
            )
        rows = jnp.where((node % width) // LANES == q, pair_row, -1)[None, :]
        next_gen, inj, price, next_c, next_d = simple_call(
            functools.partial(dispatch_kernel, q, width, parts, store_blk),
            [by_node, jax.ShapeDtypeStruct((groups, hours, LANES), f32), by_store, by_store, by_store],
            "dispatch",
            *images, dual_balance[0][:, None], gen, head, fuel_cost[None, :], chg, dis, backward,
            power_limit[None, :], rows, price, next_gen,
        )
        injs = [inj]
        for s in range(1, parts):
            injs.append(lax.ppermute(inj, "net", [(i, (i - s) % parts) for i in range(parts)]))
        tail = (line, line_base[0], line_limit[None, :]) if q == chunks - 1 else None
        flows, sums = flow_step(pattern, gathered[q], injs, flows, tail)
        totals_by_lane = totals_by_lane + sums

    next_empty, next_full = simple_call(
        level_kernel, [by_store, by_store], "levels",
        chg, dis, next_c, next_d, empty, full, loss, extra_store[None, :],
    )
    extra_generation = 2.0 * next_gen - gen
    next_headroom = jnp.maximum(head + dual_step * (extra_generation - avail * extra_plant), 0.0)
    next_balance = dual_balance + dual_step * (
        jnp.sum(totals_by_lane, axis=1)[None] / (block_count * width) - demand
    )
    return (
        next_gen[None], next_c[None], next_d[None], next_plant, next_store, next_balance,
        flows[None], next_headroom[None], next_empty[None], next_full[None],
    )


def solution(mesh):
    row = P("scen", None, "net")
    placed = (
        row, row, row, P("net"), P("net"), P("scen", None), row, row, row, row, row,
        P("scen", None), row, P("net"), P("net"), P("net"), P("net"), P("net"), P("net"), P("net"),
        P("net", "scen", None, None), P("net", None),
    )
    return jax.shard_map(
        body,
        mesh=mesh,
        in_specs=placed,
        out_specs=(row, row, row, P("net"), P("net"), P("scen", None), row, row, row, row),
        check_vma=False,
    )
```

time: 479 us -> 319 us (0.67)
  matrix products: 126 us -> 0 us
  Pallas kernels: 0 us -> 79 us
  waiting for transfers between devices: 205 us -> 133 us
  local copies, waits for them, and re-layouts: 46.8 us -> 10.5 us
  other arithmetic: 17.1 us -> 8.78 us
  starting transfers between devices: 0.12 us -> 5.55 us
    dot_general x7 -> x0, matrix products: 126 us -> none  [the longest x1 48.1 us: body(): jnp.einsum('shgpc,glpc->shgl', chosen, full_factors, precision=highest)]
    all_gather x2, waiting for transfers between devices: 199 us -> 78.3 us  [body(): gathered.append(lax.all_gather(piece, 'scen', axis=0))]
    pallas_call x0 -> x8, Pallas kernels: none -> 79 us  [the longest x2 32.9 us: flow_step(): pl.pallas_call(functools.partial(flow_kernel, slots, parts, prev is None,...]
    ppermute x0 -> x4, waiting for transfers between devices: none -> 55.2 us  [the longest x2 30.3 us: body(): lax.ppermute(partial_images[s], 'net', [(i, (i + s) % parts) for i in ran...]
    unnamed x95 -> x36, local copies, waits for them, and re-layouts: 25.5 us -> 2.78 us
    gather x1 -> x0, local copies, waits for them, and re-layouts: 6.35 us -> none  [body(): chosen = jnp.take(all_blocks, block_pattern, axis=2)]
    add x10 -> x1, other arithmetic: 6.21 us -> 0.57 us  [body(): dual_balance + dual_step * (jnp.sum(totals_by_lane, axis=1)[None] / (bloc...]
    ppermute x0 -> x4, starting transfers between devices: none -> 5.47 us  [the longest x2 2.83 us: body(): lax.ppermute(inj, 'net', [(i, (i - s) % parts) for i in range(parts)])]
  transfers between devices with their start and end apart: 3 -> 6, of which waited for: 3 -> 6; matrix products, arithmetic and copies ran while one was open for 12% -> 3% of each run, Pallas kernels for 0% -> 13%
where the time goes in v1:
time: 319 us; the launch traced here: 318 us
  waiting for transfers between devices  133 us (42%)
  Pallas kernels  79 us (25%)
  blocking collectives  66.4 us (21%)
  between operations  14.2 us (4%)
  local copies, waits for them, and re-layouts  10.5 us (3%)
  other arithmetic  8.78 us (3%)
  starting transfers between devices  5.55 us (2%)
    all_gather x2, waiting for transfers between devices, body(): gathered.append(lax.all_gather(piece, 'scen', axis=0))  78.3 us
    psum x1, blocking collectives, body(): totals = lax.psum(jnp.concatenate([plant_part, store_part]), 'scen')  66.4 us
    pallas_call x2, Pallas kernels, flow_step(): pl.pallas_call(functools.partial(flow_kernel, slots, parts, prev is None,...  32.9 us
    ppermute x2, waiting for transfers between devices, body(): lax.ppermute(partial_images[s], 'net', [(i, (i + s) % parts) for i in ran...  30.3 us
    pallas_call x2, Pallas kernels, image_parts(): pl.pallas_call(functools.partial(image_kernel, slots, parts), out_shape=[...  30.1 us
    ppermute x2, waiting for transfers between devices, body(): lax.ppermute(inj, 'net', [(i, (i - s) % parts) for i in range(parts)])  24.8 us
    pallas_call x4, Pallas kernels, simple_call(): pl.pallas_call(kernel, out_shape=out_shape, compiler_params=pltpu.Compile...  16.1 us
  transfers between devices with their start and end apart: 6, of which 6 were waited for; matrix products, arithmetic and copies ran while one was open for 3% of the time, Pallas kernels for 13%

profile of v1, /device:TPU:0, one launch (start us, length us, event | category | flops | bytes accessed | tf_op | source)
XLA Modules:
  0.0 317.9 jit_solution(5994810443848490613)
XLA Ops:
  7.2 2.0 fusion.29
  9.2 0.8 copy.39
  10.0 1.3 all_gather_reshape.7
  11.4 0.8 copy.38
  12.2 1.3 all_gather_reshape.6
  13.5 1.1 reduce_sum.28
  14.7 2.1 adjoint.1.refs_1_.refs_8_
  17.0 66.4 %psum.7.refs_0_ = f32[2560]{0:T(1024)} all-reduce(f32[2560]{0:T(1024)S(1)} %pad_maximum_fusion), channel_id=1, replica_groups=mesh['scen'=16,'net'=2] {'scen'}, use_global_device_ids=true, to_apply=%region_2.3 | all-reduce | flops 2560 | bytes 20480 | tf_op jit(solution)/shard_map/psum | solution.py:299
  84.0 40.1 %all-gather.5.cloned.1.call-done.fac = f32[16,8,32,1280]{3,2,1,0:T(8,128)} async-done(((f32[1,8,32,1280]{3,2,1,0:T(8,128)}), f32[16,8,32,1280]{3,2,1,0:T(8,128)}) %all-gather.5.cloned.1.call-update) | async-done | bytes 20971536 | tf_op jit(solution)/shard_map/all_gather | solution.py:292
  124.1 15.3 %image.2 = (f32[8,168,128]{2,1,0:T(8,128)}, f32[8,168,128]{2,1,0:T(8,128)}) custom-call(s32[8,10]{1,0:T(8,128)} %add_select_fusion.pat, f32[168,4096]{1,0:T(8,128)} %bitcast.43, f32[16,8,32,1280]{3,2,1,0:T(8,128)} %all-gather.5.cloned.1.call-done.fac, f32[2560]{0:T(1024)} %psum.7.refs_0_, f32[168,512]{1,0:T(8,128)} %adjoint.1.refs_1_.refs_8_), custom_call_target="tpu_custom_call" | custom-call | flops 5284823040 | bytes 20971520 | tf_op jit(solution)/shard_map/image/pallas_call | solution.py:77
  139.4 1.2 collective-permute-start
  140.6 0.8 copy.40.refs_2_
  142.5 14.6 %collective-permute-done.refs_1_ = f32[8,168,128]{2,1,0:T(8,128)S(1)} collective-permute-done((f32[8,168,128]{2,1,0:T(8,128)}, f32[8,168,128]{2,1,0:T(8,128)S(1)}, u32[]{:S(2)}, u32[]{:S(2)}) %collective-permute-start) | collective-permute-done | bytes 688160 | tf_op jit(solution)/shard_map/ppermute | solution.py:323
  157.1 0.8 broadcast_in_dim.56.refs_11_
  158.1 5.6 %dispatch.2 = (f32[168,2048]{1,0:T(8,128)}, f32[8,168,128]{2,1,0:T(8,128)}, f32[168,512]{1,0:T(8,128)}, f32[168,512]{1,0:T(8,128)}, f32[168,512]{1,0:T(8,128)}) custom-call(f32[8,168,128]{2,1,0:T(8,128)} %get-tuple-element.27.refs_0_, f32[8,168,128]{2,1,0:T(8,128)} %copy-done.6, f32[168,1]{1,0:T(8,128)} %copy.40.refs_2_, f32[168,2048]{1,0:T(8,128)} %bitcast.48, ...), custom_call_target="tpu_custom_call" | custom-call | flops 79926528 | bytes 9990816 | tf_op jit(solution)/shard_map/dispatch/pallas_call | solution.py:215
  163.6 1.3 collective-permute-start.1
  164.9 15.7 %collective-permute-done.1.refs_1_ = f32[8,168,128]{2,1,0:T(8,128)S(1)} collective-permute-done((f32[8,168,128]{2,1,0:T(8,128)}, f32[8,168,128]{2,1,0:T(8,128)S(1)}, u32[]{:S(2)}, u32[]{:S(2)}) %collective-permute-start.1) | collective-permute-done | bytes 688160 | tf_op jit(solution)/shard_map/ppermute | solution.py:335
  180.6 0.8 copy-done.5
  181.5 15.7 %flows.2 = (f32[168,4096]{1,0:T(8,128)}, f32[168,128]{1,0:T(8,128)}) custom-call(s32[8,10]{1,0:T(8,128)} %add_select_fusion.pat, f32[16,8,32,1280]{3,2,1,0:T(8,128)} %all-gather.5.cloned.1.call-done.fac, f32[8,168,128]{2,1,0:T(8,128)} %get-tuple-element.29.refs_0_, f32[8,168,128]{2,1,0:T(8,128)} %copy-done.5), custom_call_target="tpu_custom_call" | custom-call | flops 5284823040 | bytes 20971520 | tf_op jit(solution)/shard_map/flows/pallas_call | solution.py:156
  197.1 38.2 %all-gather.3.cloned.1.call-done.fac = f32[16,8,32,1280]{3,2,1,0:T(8,128)} async-done(((f32[1,8,32,1280]{3,2,1,0:T(8,128)}), f32[16,8,32,1280]{3,2,1,0:T(8,128)}) %all-gather.3.cloned.1.call-update) | async-done | bytes 20971536 | tf_op jit(solution)/shard_map/all_gather | solution.py:292
  235.3 14.8 %image.3 = (f32[8,168,128]{2,1,0:T(8,128)}, f32[8,168,128]{2,1,0:T(8,128)}) custom-call(s32[8,10]{1,0:T(8,128)} %add_select_fusion.pat, f32[168,4096]{1,0:T(8,128)} %bitcast.44, f32[16,8,32,1280]{3,2,1,0:T(8,128)} %all-gather.3.cloned.1.call-done.fac, f32[168,4096]{1,0:T(8,128)} %get-tuple-element.30.refs_0_.refs_2_), custom_call_target="tpu_custom_call" | custom-call | flops 5284823040 | bytes 20971520 | tf_op jit(solution)/shard_map/image/pallas_call | solution.py:77
  250.1 1.5 collective-permute-start.2
  252.2 15.7 %collective-permute-done.2.refs_1_ = f32[8,168,128]{2,1,0:T(8,128)S(1)} collective-permute-done((f32[8,168,128]{2,1,0:T(8,128)}, f32[8,168,128]{2,1,0:T(8,128)S(1)}, u32[]{:S(2)}, u32[]{:S(2)}) %collective-permute-start.2) | collective-permute-done | bytes 688160 | tf_op jit(solution)/shard_map/ppermute | solution.py:323
  267.9 0.9 copy-done.7
  268.8 5.6 %dispatch.3 = (f32[168,2048]{1,0:T(8,128)}, f32[8,168,128]{2,1,0:T(8,128)}, f32[168,512]{1,0:T(8,128)}, f32[168,512]{1,0:T(8,128)}, f32[168,512]{1,0:T(8,128)}) custom-call(f32[8,168,128]{2,1,0:T(8,128)} %get-tuple-element.31.refs_0_, f32[8,168,128]{2,1,0:T(8,128)} %copy-done.7, f32[168,1]{1,0:T(8,128)} %copy.40.refs_2_, f32[168,2048]{1,0:T(8,128)} %bitcast.50, ...), custom_call_target="tpu_custom_call" | custom-call | flops 79926528 | bytes 9990816 | tf_op jit(solution)/shard_map/dispatch/pallas_call | solution.py:215
  274.4 1.5 collective-permute-start.3
  276.5 2.8 levels.1
  279.3 2.9 fusion.5
  282.2 9.2 %collective-permute-done.3.refs_1_ = f32[8,168,128]{2,1,0:T(8,128)S(1)} collective-permute-done((f32[8,168,128]{2,1,0:T(8,128)}, f32[8,168,128]{2,1,0:T(8,128)S(1)}, u32[]{:S(2)}, u32[]{:S(2)}) %collective-permute-start.3) | collective-permute-done | bytes 688160 | tf_op jit(solution)/shard_map/ppermute | solution.py:335
  291.4 0.9 copy-done.4
  292.3 17.2 %flows.3 = (f32[168,4096]{1,0:T(8,128)}, f32[168,128]{1,0:T(8,128)}) custom-call(s32[8,10]{1,0:T(8,128)} %add_select_fusion.pat, f32[16,8,32,1280]{3,2,1,0:T(8,128)} %all-gather.3.cloned.1.call-done.fac, f32[8,168,128]{2,1,0:T(8,128)} %get-tuple-element.39.refs_0_, f32[8,168,128]{2,1,0:T(8,128)} %copy-done.4, f32[168,4096]{1,0:T(8,128)} %get-tuple-element.30.refs_0_.refs_2_, ...), custom_call_target="tpu_custom_call" | custom-call | flops 5284823040 | bytes 20971520 | tf_op jit(solution)/shard_map/flows/pallas_call | solution.py:156
  309.5 1.0 add_reduce_fusion
  (46 shorter events, 4.0 us)
Async XLA Ops:
  7.2 116.9 %all-gather.5.cloned.1.call-start = ((), (), s32[]{:S(2)}) async-start(), calls=%async_computation.1 | async-start | bytes 22282240 | tf_op jit(solution)/shard_map/all_gather | solution.py:292
  11.4 223.9 %all-gather.3.cloned.1.call-start = ((), (), s32[]{:S(2)}) async-start(), calls=%async_computation | async-start | bytes 22282240 | tf_op jit(solution)/shard_map/all_gather | solution.py:292
  12.2 4.6 %copy-start.3 = (f32[1,168,2048]{2,1,0:T(8,128)S(1)}, f32[1,168,2048]{2,1,0:T(8,128)}, u32[]{:S(2)}) copy-start(f32[1,168,2048]{2,1,0:T(8,128)} %param.32) | copy-start | bytes 4128772
  13.5 3.3 %copy-start = (f32[1,168,2048]{2,1,0:T(8,128)S(1)}, f32[1,168,2048]{2,1,0:T(8,128)}, u32[]{:S(2)}) copy-start(f32[1,168,2048]{2,1,0:T(8,128)} %param.29) | copy-start | bytes 4128772
  16.8 66.6 %copy-start.13 = (s32[8,10]{1,0:T(8,128)S(1)}, s32[8,10]{1,0:T(8,128)}, u32[]{:S(2)}) copy-start(s32[8,10]{1,0:T(8,128)} %param.43) | copy-start | bytes 964
  124.1 16.5 %copy-start.12 = (f32[1,168]{1,0:T(1,128)S(1)}, f32[1,168]{1,0:T(1,128)}, u32[]{:S(2)}) copy-start(f32[1,168]{1,0:T(1,128)} %param.27) | copy-start | bytes 2020
  124.1 17.2 %copy-start.14 = (s32[512]{0:T(512)S(1)}, s32[512]{0:T(512)}, u32[]{:S(2)}) copy-start(s32[512]{0:T(512)} %param.41) | copy-start | bytes 6148
  139.4 17.7 %collective-permute-start = (f32[8,168,128]{2,1,0:T(8,128)}, f32[8,168,128]{2,1,0:T(8,128)S(1)}, u32[]{:S(2)}, u32[]{:S(2)}) collective-permute-start(f32[8,168,128]{2,1,0:T(8,128)} %get-tuple-element.28), channel_id=1, source_target_pairs={{0,1},{1,0},{2,3},{3,2},{4,5},{5,4},{6,7},{7,6},{8,9},{9,8},{10,11... | collective-permute-start | bytes 2064392 | tf_op jit(solution)/shard_map/ppermute | solution.py:323
  157.1 1.0 copy-start.6
  163.6 17.0 %collective-permute-start.1 = (f32[8,168,128]{2,1,0:T(8,128)}, f32[8,168,128]{2,1,0:T(8,128)S(1)}, u32[]{:S(2)}, u32[]{:S(2)}) collective-permute-start(f32[8,168,128]{2,1,0:T(8,128)} %get-tuple-element.29.refs_0_), channel_id=1, source_target_pairs={{0,1},{1,0},{2,3},{3,2},{4,5},{5,4},{6,7},{7,6},{8,9},{9,8},{10,11... | collective-permute-start | bytes 2064392 | tf_op jit(solution)/shard_map/ppermute | solution.py:335
  180.6 0.8 copy-start.5
  235.3 16.3 %copy-start.8 = (f32[2560]{0:T(1024)S(1)}, f32[2560]{0:T(1024)}, u32[]{:S(2)}) copy-start(f32[2560]{0:T(1024)} %psum.7.refs_0_) | copy-start | bytes 30724
  235.3 16.3 %copy-start.10 = (f32[2048]{0:T(1024)S(1)}, f32[2048]{0:T(1024)}, u32[]{:S(2)}) copy-start(f32[2048]{0:T(1024)} %param.25) | copy-start | bytes 24580
  235.3 16.3 %copy-start.11 = (f32[2048]{0:T(1024)S(1)}, f32[2048]{0:T(1024)}, u32[]{:S(2)}) copy-start(f32[2048]{0:T(1024)} %param.37) | copy-start | bytes 24580
  250.1 17.8 %collective-permute-start.2 = (f32[8,168,128]{2,1,0:T(8,128)}, f32[8,168,128]{2,1,0:T(8,128)S(1)}, u32[]{:S(2)}, u32[]{:S(2)}) collective-permute-start(f32[8,168,128]{2,1,0:T(8,128)} %get-tuple-element.32), channel_id=1, source_target_pairs={{0,1},{1,0},{2,3},{3,2},{4,5},{5,4},{6,7},{7,6},{8,9},{9,8},{10,11... | collective-permute-start | bytes 2064392 | tf_op jit(solution)/shard_map/ppermute | solution.py:323
  267.9 0.9 copy-start.7
  268.8 7.2 %copy-start.15 = (f32[512]{0:T(512)S(1)}, f32[512]{0:T(512)}, u32[]{:S(2)}) copy-start(f32[512]{0:T(512)} %param.26) | copy-start | bytes 6148
  268.8 7.2 %copy-start.16 = (f32[512]{0:T(512)S(1)}, f32[512]{0:T(512)}, u32[]{:S(2)}) copy-start(f32[512]{0:T(512)} %param.38) | copy-start | bytes 6148
  268.8 10.5 %copy-start.2 = (f32[1,168,2048]{2,1,0:T(8,128)S(1)}, f32[1,168,2048]{2,1,0:T(8,128)}, u32[]{:S(2)}) copy-start(f32[1,168,2048]{2,1,0:T(8,128)} %param.22) | copy-start | bytes 4128772
  274.4 4.9 %copy-start.1 = (f32[1,168,2048]{2,1,0:T(8,128)S(1)}, f32[1,168,2048]{2,1,0:T(8,128)}, u32[]{:S(2)}) copy-start(f32[1,168,2048]{2,1,0:T(8,128)} %param.29) | copy-start | bytes 4128772
  274.4 17.0 %collective-permute-start.3 = (f32[8,168,128]{2,1,0:T(8,128)}, f32[8,168,128]{2,1,0:T(8,128)S(1)}, u32[]{:S(2)}, u32[]{:S(2)}) collective-permute-start(f32[8,168,128]{2,1,0:T(8,128)} %get-tuple-element.39.refs_0_), channel_id=1, source_target_pairs={{0,1},{1,0},{2,3},{3,2},{4,5},{5,4},{6,7},{7,6},{8,9},{9,8},{10,11... | collective-permute-start | bytes 2064392 | tf_op jit(solution)/shard_map/ppermute | solution.py:335
  291.4 0.9 copy-start.4
  292.3 17.2 %copy-start.9 = (f32[168,128]{1,0:T(8,128)S(1)}, f32[168,128]{1,0:T(8,128)}, u32[]{:S(2)}) copy-start(f32[168,128]{1,0:T(8,128)} %get-tuple-element.38) | copy-start | bytes 258052
  292.3 18.2 %copy-start.17 = (f32[1,168]{1,0:T(1,128)S(1)}, f32[1,168]{1,0:T(1,128)}, u32[]{:S(2)}) copy-start(f32[1,168]{1,0:T(1,128)} %param.33) | copy-start | bytes 2020
Sparse Core Ops, SparseCore 0:
  11.5 112.5 all-gather.4
  126.3 108.9 all-gather.2
